TPU v7x, 512 devices: a whole 4x4x16 slice. The times are simulated.
512 devices in a mesh: segment: 4 (over x_hi, core), seq: 32 (over x_lo, z), dp: 4 (over y).
Axes of the slice: x: 4 (x_hi: 2, x_lo: 2; x = x_hi * 2 + x_lo), y: 4, z: 16, core: 2. Of those that a mesh axis runs over, the one named last changes fastest.
Arguments:
- q_in: bfloat16 [4, 4096, 1536], P('dp', 'seq', 'segment'), may hold values from -128 to 128
- k_in: bfloat16 [4, 4096, 1536], P('dp', 'seq', 'segment'), may hold values from -128 to 128
- v_in: bfloat16 [4, 4096, 1536], P('dp', 'seq', 'segment'), may hold values from -6 to 6
- q_gain: float32 [2, 64], replicated, may hold values from 1.5 to 4
- gate: float32 [768], replicated, may hold values from -6 to 6
- cot: bfloat16 [4, 4096, 768], P('dp', 'seq'), may hold values from -6 to 6
Outputs:
- attn_out: bfloat16 [4, 4096, 1536], P('dp', 'seq', 'segment')
- grad_gate: float32 [768], replicated
All inputs are finite; a program needn't handle non-finite values.
Results may differ from a plain program's by a relative error of at most 0.028.
The roundings to bfloat16 on the way count: a program that leaves them out, or rounds other values in their place, can miss the bound.
Values may be sent and summed in bfloat16 or wider, within the bound.
A program may use at most 64 MiB of HBM per device.

v0:
```python
import jax
import jax.numpy as jnp
from jax import lax
from jax.sharding import PartitionSpec as P

HEAD_DIM = 64


def shifted(value, axis, steps):
    count = lax.axis_size(axis)
    first, last = (max(0, -steps), min(count, count - steps))
    return lax.ppermute(value, axis, [(source, source + steps) for source in range(first, last)])


def attend(query, all_keys, all_values):
    count_rows = query.shape[0]
    total_keys = all_keys.shape[0]
    span = 2 * HEAD_DIM
    pieces = []
    probs_list = []
    totals_list = []
    for offset in range(0, query.shape[1], span):
        query_group = query[:, offset : offset + span].reshape(count_rows, 2, HEAD_DIM)
        keys_group = all_keys[:, offset : offset + span].reshape(total_keys, 2, HEAD_DIM)
        values_group = all_values[:, offset : offset + span].reshape(total_keys, 2, HEAD_DIM)
        scores = jnp.einsum(
            "qhd,khd->hqk", query_group, keys_group, preferred_element_type=jnp.float32
        ) * HEAD_DIM ** (-0.5)
        peak = jnp.max(scores, axis=-1, keepdims=True)
        expd = jnp.exp(scores - peak)
        total = jnp.sum(expd, axis=-1, keepdims=True)
        probs = expd.astype(jnp.bfloat16)
        result = jnp.einsum("hqk,khd->qhd", probs, values_group, preferred_element_type=jnp.float32)
        result = result / jnp.transpose(total, (1, 0, 2))
        pieces.append(result.reshape(count_rows, span))
        probs_list.append(probs)
        totals_list.append(total)
    return (jnp.concatenate(pieces, axis=1), probs_list, totals_list)


def attend_back(probs_list, totals_list, normed, upstream, all_keys, all_values):
    count_rows = upstream.shape[0]
    total_keys = all_keys.shape[0]
    span = 2 * HEAD_DIM
    pieces = []
    for number in range(len(probs_list)):
        offset = number * span
        upstream_group = upstream[:, offset : offset + span].reshape(count_rows, 2, HEAD_DIM)
        normed_group = normed[:, offset : offset + span].reshape(count_rows, 2, HEAD_DIM)
        keys_group = all_keys[:, offset : offset + span].reshape(total_keys, 2, HEAD_DIM)
        values_group = all_values[:, offset : offset + span].reshape(total_keys, 2, HEAD_DIM)
        dprob = jnp.einsum(
            "qhd,khd->hqk", upstream_group, values_group, preferred_element_type=jnp.float32
        )
        delta = jnp.sum(upstream_group.astype(jnp.float32) * normed_group, axis=-1)
        delta = jnp.transpose(delta, (1, 0))[:, :, None]
        dscore = (
            probs_list[number].astype(jnp.float32) / totals_list[number] * (dprob - delta)
        ).astype(jnp.bfloat16)
        result = jnp.einsum(
            "hqk,khd->qhd", dscore, keys_group, preferred_element_type=jnp.float32
        ) * HEAD_DIM ** (-0.5)
        pieces.append(result.reshape(count_rows, span))
    return jnp.concatenate(pieces, axis=1)


def local(q_in, k_in, v_in, q_gain, gate, cot):
    half = lax.axis_size("segment") // 2
    place = lax.axis_index("segment")
    is_main = place >= half
    section = place // half
    slot = place % half
    queries = q_in[0]
    keys = k_in[0]
    values = v_in[0]
    count_rows = queries.shape[0]
    width_dev = queries.shape[1]
    all_keys, all_values = (
        lax.all_gather(keys, "seq", axis=0, tiled=True),
        lax.all_gather(values, "seq", axis=0, tiled=True),
    )
    gain_row = lax.dynamic_slice_in_dim(q_gain, section, 1, 0)[0]
    gate_part = lax.dynamic_slice_in_dim(gate, slot * width_dev, width_dev, 0)
    cot_part = lax.dynamic_slice_in_dim(cot[0], slot * width_dev, width_dev, 1)
    raw = queries.astype(jnp.float32).reshape(count_rows, width_dev // HEAD_DIM, HEAD_DIM)
    unit = raw * lax.rsqrt(jnp.mean(raw * raw, axis=-1, keepdims=True) + 1e-06)
    base = (unit * gain_row).reshape(count_rows, width_dev)

    def control_run(base_in):
        normed_c = attend(base_in.astype(jnp.bfloat16), all_keys, all_values)[0]
        return lax.optimization_barrier(normed_c.astype(jnp.bfloat16))

    def control_skip(base_in):
        return jnp.zeros((count_rows, width_dev), jnp.bfloat16)

    first = lax.cond(is_main, control_skip, control_run, base)
    first_wide = first.astype(jnp.float32)
    outgoing = (gate_part * first_wide).astype(jnp.bfloat16)
    incoming = shifted(outgoing, "segment", half)

    def main_run(incoming_in):
        query = (base + incoming_in.astype(jnp.float32)).astype(jnp.bfloat16)
        normed_m, probs_list, totals_list = attend(query, all_keys, all_values)
        dquery = attend_back(probs_list, totals_list, normed_m, cot_part, all_keys, all_values)
        return (normed_m.astype(jnp.bfloat16), dquery)

    def main_skip(incoming_in):
        return (
            jnp.zeros((count_rows, width_dev), jnp.bfloat16),
            jnp.zeros((count_rows, width_dev), jnp.float32),
        )

    final, dquery_main = lax.cond(is_main, main_run, main_skip, incoming)
    returned = shifted(dquery_main.astype(jnp.bfloat16), "segment", -half)
    returned_wide = returned.astype(jnp.float32)
    part_gate = jnp.sum(first_wide * returned_wide, axis=0)
    placed = lax.dynamic_update_slice_in_dim(
        jnp.zeros((width_dev * half,), jnp.float32), part_gate, slot * width_dev, 0
    )
    total_gate = lax.psum(placed, ("segment", "seq", "dp"))
    output = jnp.where(is_main, final, first)
    return (output[None], total_gate)


def solution(mesh):
    in_specs = (
        P("dp", "seq", "segment"),
        P("dp", "seq", "segment"),
        P("dp", "seq", "segment"),
        P(),
        P(),
        P("dp", "seq", None),
    )
    out_specs = (P("dp", "seq", "segment"), P())
    return jax.shard_map(local, mesh=mesh, in_specs=in_specs, out_specs=out_specs, check_vma=False)
```

profile of v0, /device:TPU:1, one launch (start us, length us, event | category | flops | bytes accessed | tf_op | source)
XLA Modules:
  0.0 449.7 jit_solution(1224437534765963869)
XLA Ops:
  7.2 0.0 copy-start
  7.2 0.0 all-gather.5.cloned.1.call-start
  7.2 1.6 copy.10
  8.9 0.0 all-gather.5.cloned.1.call-update
  8.9 0.0 all-gather.7.cloned.1.call-start
  8.9 1.6 copy.11
  10.6 0.0 all-gather.7.cloned.1.call-update
  10.6 0.0 copy-done
  10.6 0.1 mul.127
  10.7 1.0 copy.9
  11.8 0.1 fusion.70
  11.9 0.8 dynamic_slice.11
  12.7 116.3 %all-gather.5.cloned.1.call-done = bf16[1,4096,384]{1,2,0:T(8,128)(2,1)} async-done(((bf16[1,128,384]{1,2,0:T(8,128)(2,1)}), bf16[1,4096,384]{1,2,0:T(8,128)(2,1)}) %all-gather.5.cloned.1.call-update) | async-done | bytes 3145744 | tf_op jit(solution)/shard_map/all_gather | solution.py:79
  129.0 133.1 %all-gather.7.cloned.1.call-done = bf16[1,4096,384]{1,2,0:T(8,128)(2,1)} async-done(((bf16[1,128,384]{1,2,0:T(8,128)(2,1)}), bf16[1,4096,384]{1,2,0:T(8,128)(2,1)}) %all-gather.7.cloned.1.call-update) | async-done | bytes 3145744 | tf_op jit(solution)/shard_map/all_gather | solution.py:80
  262.1 10.9 %conditional.2 = (f32[128,384]{0,1:T(8,128)S(1)}, bf16[128,384]{1,0:T(8,128)(2,1)S(1)}) conditional(s32[]{:T(128)} %convert_element_type.105, (f32[128,384]{0,1:T(8,128)S(1)}, bf16[4096,384]{0,1:T(8,128)(2,1)}, bf16[4096,384]{0,1:T(8,128)(2,1)}) %tuple.81, () %tuple.30), branch_computations={%region_1.8_spmd, %region_8.9_spmd} | conditional | flops 824670720 | bytes 58014736 | solution.py:96
  262.1 3.2 fusion.71
  265.4 0.8 fusion.76
  266.2 0.7 fusion
  267.0 0.9 fusion.39
  267.9 0.8 fusion.75
  268.7 0.7 fusion.2
  269.4 0.9 fusion.36
  270.4 0.8 fusion.74
  271.2 0.7 fusion.4
  271.9 0.9 fusion.33
  272.9 0.1 copy.15
  273.1 0.0 copy-start.6
  273.1 0.1 multiply_convert_fusion
  273.2 1.3 collective-permute-start
  274.5 1.6 collective-permute-done
  276.1 0.0 copy-done.6
  276.1 0.9 conditional.3
  276.1 0.7 broadcast.53.clone
  277.0 1.3 collective-permute-start.1
  278.3 1.6 select_bitcast_fusion
  279.8 38.2 %collective-permute-done.1 = bf16[128,384]{0,1:T(8,128)(2,1)S(1)} collective-permute-done((bf16[128,384]{0,1:T(8,128)(2,1)S(1)}, bf16[128,384]{0,1:T(8,128)(2,1)S(1)}, u32[]{:S(2)}, u32[]{:S(2)}) %collective-permute-start.1) | collective-permute-done | bytes 98336 | tf_op jit(solution)/shard_map/ppermute | solution.py:12
  318.0 0.1 multiply_reduce_fusion.3
  318.2 0.2 dynamic_update_slice.3
  318.5 124.4 %psum.7 = f32[768]{0:T(1024)} all-reduce(f32[768]{0:T(1024)S(1)} %dynamic_update_slice.3), channel_id=1, replica_groups=mesh['segment'=4,'seq'=32,'dp'=4] {'segment','seq','dp'}, use_global_device_ids=true, to_apply=%region_21.22 | all-reduce | flops 768 | bytes 6144 | tf_op jit(solution)/shard_map/psum | solution.py:120
  (11 shorter events, 0.1 us)
Async XLA Ops:
  7.2 3.4 copy-start
  7.2 121.8 %all-gather.5.cloned.1.call-start = ((), (), s32[]{:S(2)}) async-start(), calls=%async_computation | async-start | bytes 3244032 | tf_op jit(solution)/shard_map/all_gather | solution.py:79
  8.9 253.3 %all-gather.7.cloned.1.call-start = ((), (), s32[]{:S(2)}) async-start(), calls=%async_computation.1 | async-start | bytes 3244032 | tf_op jit(solution)/shard_map/all_gather | solution.py:80
  273.1 3.1 copy-start.6
  273.2 2.9 collective-permute-start
  277.0 41.1 %collective-permute-start.1 = (bf16[128,384]{0,1:T(8,128)(2,1)S(1)}, bf16[128,384]{0,1:T(8,128)(2,1)S(1)}, u32[]{:S(2)}, u32[]{:S(2)}) collective-permute-start(bf16[128,384]{0,1:T(8,128)(2,1)S(1)} %get-tuple-element.53), channel_id=1, source_target_pairs={{256,0},{384,128},{257,1},{385,129},{258,2},{386,130},{259,3},{387... | collective-permute-start | bytes 294920 | tf_op jit(solution)/shard_map/ppermute | solution.py:12
Sparse Core Ops, SparseCore 0:
  10.6 118.3 all-gather.4
  131.0 131.0 all-gather.6
where the time goes:
time: 450 us
  waiting for transfers between devices  289 us (64%)
  blocking collectives  124 us (28%)
  between operations  14.2 us (3%)
  local copies, waits for them, and re-layouts  9.4 us (2%)
  matrix products  5.29 us (1%)
    all_gather x1, waiting for transfers between devices, local(): lax.all_gather(values, 'seq', axis=0, tiled=True)  133 us
    psum x1, blocking collectives, local(): total_gate = lax.psum(placed, ('segment', 'seq', 'dp'))  124 us
    all_gather x1, waiting for transfers between devices, local(): lax.all_gather(keys, 'seq', axis=0, tiled=True)  116 us
    ppermute x2, waiting for transfers between devices, shifted(): lax.ppermute(value, axis, [(source, source + steps) for source in range(f...  39.8 us
  transfers between devices with their start and end apart: 4, of which 4 were waited for; matrix products, arithmetic and copies ran while one was open for 1% of the time, Pallas kernels for 0%

commit v1 on v0

--- a/solution.py
+++ b/solution.py
@@ -117,7 +117,7 @@
     placed = lax.dynamic_update_slice_in_dim(
         jnp.zeros((width_dev * half,), jnp.float32), part_gate, slot * width_dev, 0
     )
-    total_gate = lax.psum(placed, ("segment", "seq", "dp"))
+    total_gate = jnp.sum(lax.all_gather(placed, ("segment", "seq", "dp")), axis=0)
     output = jnp.where(is_main, final, first)
     return (output[None], total_gate)
 

time: 450 us -> 1400 us (3.11)
  waiting for transfers between devices: 289 us -> 1360 us
  blocking collectives: 124 us -> 0 us
    all_gather x0 -> x1, waiting for transfers between devices: none -> 1070 us  [local(): lax.all_gather(placed, ('segment', 'seq', 'dp'))]
    psum x1 -> x0, blocking collectives: 124 us -> none  [local(): total_gate = lax.psum(placed, ('segment', 'seq', 'dp'))]
  transfers between devices with their start and end apart: 4 -> 5, of which waited for: 4 -> 5; matrix products, arithmetic and copies ran while one was open for 1% -> 0% of each run, Pallas kernels for 0% -> 0%
where the time goes in v1:
time: 1400 us
  waiting for transfers between devices  1360 us (97%)
    all_gather x1, waiting for transfers between devices, local(): lax.all_gather(placed, ('segment', 'seq', 'dp'))  1070 us
    all_gather x1, waiting for transfers between devices, local(): lax.all_gather(values, 'seq', axis=0, tiled=True)  133 us
    all_gather x1, waiting for transfers between devices, local(): lax.all_gather(keys, 'seq', axis=0, tiled=True)  116 us
    ppermute x2, waiting for transfers between devices, shifted(): lax.ppermute(value, axis, [(source, source + steps) for source in range(f...  41.4 us
  transfers between devices with their start and end apart: 5, of which 5 were waited for; matrix products, arithmetic and copies ran while one was open for 0% of the time, Pallas kernels for 0%

profile of v1, /device:TPU:1, one launch (start us, length us, event | category | flops | bytes accessed | tf_op | source)
XLA Modules:
  0.0 1396.9 jit_solution(6211296602821093177)
XLA Ops:
  7.2 0.0 copy-start
  7.2 0.0 all-gather.7.cloned.1.call-start
  7.2 1.6 copy.16
  8.9 0.0 all-gather.7.cloned.1.call-update
  8.9 0.0 all-gather.9.cloned.1.call-start
  8.9 1.6 copy.17
  10.6 0.0 all-gather.9.cloned.1.call-update
  10.6 0.0 all-gather.11.cloned.1.call-start
  10.7 0.0 copy-done
  10.7 0.1 mul.127
  10.8 1.0 copy.15
  11.9 0.1 fusion.70
  12.0 0.8 dynamic_slice.11
  12.8 116.3 %all-gather.7.cloned.1.call-done = bf16[1,4096,384]{1,2,0:T(8,128)(2,1)} async-done(((bf16[1,128,384]{1,2,0:T(8,128)(2,1)}), bf16[1,4096,384]{1,2,0:T(8,128)(2,1)}) %all-gather.7.cloned.1.call-update) | async-done | bytes 3145744 | tf_op jit(solution)/shard_map/all_gather | solution.py:79
  129.0 133.1 %all-gather.9.cloned.1.call-done = bf16[1,4096,384]{1,2,0:T(8,128)(2,1)} async-done(((bf16[1,128,384]{1,2,0:T(8,128)(2,1)}), bf16[1,4096,384]{1,2,0:T(8,128)(2,1)}) %all-gather.9.cloned.1.call-update) | async-done | bytes 3145744 | tf_op jit(solution)/shard_map/all_gather | solution.py:80
  262.1 10.9 conditional.2
  262.1 3.2 fusion.71
  265.4 0.8 fusion.76
  266.2 0.7 fusion
  267.0 0.9 fusion.39
  267.9 0.8 fusion.75
  268.7 0.7 fusion.2
  269.4 0.9 fusion.36
  270.4 0.8 fusion.74
  271.2 0.7 fusion.4
  271.9 0.9 fusion.33
  272.9 0.1 copy.21
  273.1 0.0 copy-start.6
  273.1 0.1 multiply_convert_fusion
  273.2 1.3 collective-permute-start
  274.5 1.6 collective-permute-done
  276.1 0.0 copy-done.6
  276.1 0.9 conditional.3
  276.1 0.7 broadcast.54.clone
  277.0 1.3 collective-permute-start.1
  278.3 39.8 %collective-permute-done.1 = bf16[128,384]{0,1:T(8,128)(2,1)S(1)} collective-permute-done((bf16[128,384]{0,1:T(8,128)(2,1)S(1)}, bf16[128,384]{0,1:T(8,128)(2,1)S(1)}, u32[]{:S(2)}, u32[]{:S(2)}) %collective-permute-start.1) | collective-permute-done | bytes 98336 | tf_op jit(solution)/shard_map/ppermute | solution.py:12
  318.0 0.1 multiply_reduce_fusion.3
  318.2 0.0 copy-start.8
  318.2 0.6 copy-done.8
  318.8 0.0 all-gather.11.cloned.1.call-update
  318.8 1.6 select_bitcast_fusion
  320.4 1067.1 %all-gather.11.cloned.1.call-done = f32[512,1,768]{2,1,0:T(1,128)} async-done(((f32[1,1,768]{2,1,0:T(1,128)}), f32[512,1,768]{2,1,0:T(1,128)}) %all-gather.11.cloned.1.call-update) | async-done | bytes 1572880 | tf_op jit(solution)/shard_map/all_gather | solution.py:120
  1387.4 2.9 reduce_sum.116
  (12 shorter events, 0.1 us)
Async XLA Ops:
  7.2 3.5 copy-start
  7.2 121.8 %all-gather.7.cloned.1.call-start = ((), (), s32[]{:S(2)}) async-start(), calls=%async_computation | async-start | bytes 3244032 | tf_op jit(solution)/shard_map/all_gather | solution.py:79
  8.9 253.3 %all-gather.9.cloned.1.call-start = ((), (), s32[]{:S(2)}) async-start(), calls=%async_computation.1 | async-start | bytes 3244032 | tf_op jit(solution)/shard_map/all_gather | solution.py:80
  10.6 1376.9 %all-gather.11.cloned.1.call-start = ((), (), s32[]{:S(2)}) async-start(), calls=%async_computation.2 | async-start | bytes 1575936 | tf_op jit(solution)/shard_map/all_gather | solution.py:120
  273.1 3.1 copy-start.6
  273.2 2.9 collective-permute-start
  277.0 41.1 %collective-permute-start.1 = (bf16[128,384]{0,1:T(8,128)(2,1)S(1)}, bf16[128,384]{0,1:T(8,128)(2,1)S(1)}, u32[]{:S(2)}, u32[]{:S(2)}) collective-permute-start(bf16[128,384]{0,1:T(8,128)(2,1)S(1)} %get-tuple-element.53), channel_id=1, source_target_pairs={{256,0},{384,128},{257,1},{385,129},{258,2},{386,130},{259,3},{387... | collective-permute-start | bytes 294920 | tf_op jit(solution)/shard_map/ppermute | solution.py:12
  318.2 0.6 copy-start.8
Sparse Core Ops, SparseCore 0:
  10.6 118.3 all-gather.6
  131.0 131.0 all-gather.8
  318.9 1068.4 all-gather.10
